TPU v7x, 512 devices: a whole 4x8x8 slice. The times are simulated.
512 devices in a mesh: region: 8 (over z_hi, core), shard: 64 (over z_lo, x, y).
Axes of the slice: x: 4, y: 8, z: 8 (z_hi: 4, z_lo: 2; z = z_hi * 2 + z_lo), core: 2. Of those that a mesh axis runs over, the one named last changes fastest.
Arguments:
- points: bfloat16 [49152, 8, 128], P(('region', 'shard')), may hold values from -12 to 12
- block_owner: int32 [49152, 1], P(('region', 'shard')), may hold values from 0 to 63; in each aligned block of 96 rows (0 to 95, 96 to 191, ...) at most 3 rows name the same one
- block_node: int32 [49152], P(('region', 'shard')), may hold values from 0 to 1
- queries: bfloat16 [131072, 128], P(('region', 'shard')), may hold values from -240 to 240
- w_in: bfloat16 [128, 768], replicated, may hold values from -0.5 to 0.5
- w_key: bfloat16 [768, 768], replicated, may hold values from -0.21875 to 0.21875
- w_value: bfloat16 [768, 768], replicated, may hold values from -0.21875 to 0.21875
- w_query: bfloat16 [128, 768], replicated, may hold values from -0.5 to 0.5
- w_out: bfloat16 [768, 128], replicated, may hold values from -0.21875 to 0.21875
Outputs:
- readout: bfloat16 [131072, 128], P(('region', 'shard'))
Inputs may be any that keep to these rules, and one draw needn't show every extreme that they name: `block_owner`: among the 96 blocks of one device no shard is named more than 3 times, and some device names one shard exactly 3 times.
All inputs are finite; a program needn't handle non-finite values.
Results may differ from a plain program's by a relative error of at most 0.018.
Values may be sent and summed in bfloat16 or wider, within the bound.
No kernel may reach another device: no remote copies, remote signals or barrier semaphores. Data moves between devices by JAX's collectives and lax.ppermute only.
A program may use at most 64 MiB of HBM per device.

v0:
```python
import math
import jax
import jax.numpy as jnp
from jax import lax
from jax.sharding import PartitionSpec as P

HEADS = 12
HEAD_DIM = 64
S_DEV = 2


def layer_norm(pooled):
    mean = jnp.mean(pooled, axis=-1, keepdims=True)
    centred = pooled - mean
    spread = jnp.mean(centred * centred, axis=-1, keepdims=True)
    return (centred * lax.rsqrt(spread + 1e-05)).astype(jnp.bfloat16)


def block_ranks(owner_shard, shard_count):
    onehot = (owner_shard[..., None] == jnp.arange(shard_count, dtype=jnp.int32)).astype(jnp.int32)
    before = jnp.cumsum(onehot, axis=-2) - onehot
    return jnp.sum(before * onehot, axis=-1)


def body(points, block_owner, block_node, queries, w_in, w_key, w_value, w_query, w_out):
    shard_count = lax.axis_size("shard")
    block_count, block_points, in_features = points.shape
    model_width = w_in.shape[1]
    capacity = max(2, 2 * block_count // shard_count)
    owner_shard = block_owner[:, 0]
    routing = lax.all_gather(
        jnp.stack([owner_shard, block_node], axis=1), "shard", axis=0, tiled=True
    )
    routing = routing.reshape(shard_count, block_count, 2)
    every_owner = routing[:, :, 0]
    every_node = routing[:, :, 1]
    this_shard = lax.axis_index("shard")
    position = jnp.arange(shard_count, dtype=jnp.int32)[:, None] * capacity + block_ranks(
        every_owner, shard_count
    )
    arrives_here = every_owner == this_shard
    node_onehot = (
        (every_node[..., None] == jnp.arange(S_DEV, dtype=jnp.int32)) & arrives_here[..., None]
    ).astype(jnp.float32)
    node_onehot = node_onehot.reshape(shard_count * block_count, S_DEV)
    slot_onehot = (
        position.reshape(-1)[:, None]
        == jnp.arange(shard_count * capacity, dtype=jnp.int32)[None, :]
    ).astype(jnp.float32)
    assign = jnp.dot(node_onehot.T, slot_onehot, precision=lax.Precision.HIGHEST)
    slot_index = owner_shard * capacity + block_ranks(owner_shard, shard_count)
    outgoing = (
        jnp.zeros((shard_count * capacity, block_points, in_features), points.dtype)
        .at[slot_index]
        .set(points)
    )
    outgoing = outgoing.reshape(shard_count, capacity, block_points, in_features)
    messages = jax.nn.gelu(
        jnp.einsum(
            "jkpc,cd->jkpd",
            lax.all_to_all(outgoing, "shard", split_axis=0, concat_axis=0, tiled=True),
            w_in,
            preferred_element_type=jnp.float32,
        )
    ).astype(jnp.bfloat16)
    per_slot = messages.reshape(shard_count * capacity, block_points * model_width)
    pooled = jnp.dot(assign.astype(jnp.bfloat16), per_slot, preferred_element_type=jnp.float32)
    pooled = jnp.sum(pooled.reshape(S_DEV, block_points, model_width), axis=1)
    normed = layer_norm(pooled)
    query_count = queries.shape[0]
    query_vec = jnp.dot(queries, w_query, preferred_element_type=jnp.float32).astype(jnp.bfloat16)
    query_heads = query_vec.reshape(query_count, HEADS, HEAD_DIM)
    score_scale = HEAD_DIM ** (-0.5)
    starting = (
        jnp.full((query_count, HEADS), -1e30, jnp.float32),
        jnp.zeros((query_count, HEADS), jnp.float32),
        jnp.zeros((query_count, HEADS, HEAD_DIM), jnp.float32),
    )
    key_rows = jnp.dot(normed, w_key, preferred_element_type=jnp.float32).astype(jnp.bfloat16)
    value_rows = jnp.dot(normed, w_value, preferred_element_type=jnp.float32).astype(jnp.bfloat16)
    anchor_rows = jnp.concatenate([key_rows, value_rows], axis=1)
    region_rows = lax.all_gather(anchor_rows, "shard", axis=0, tiled=True)
    key_values = lax.all_gather(region_rows, "region", axis=0, tiled=True)
    row_count = key_values.shape[0]
    step_rows = math.gcd(row_count, 256)

    def one_block(block_index, carried):
        peak_now, denominator, numerator = carried
        block_rows = lax.dynamic_slice_in_dim(key_values, block_index * step_rows, step_rows, 0)
        key_block = block_rows[:, :model_width].reshape(step_rows, HEADS, HEAD_DIM)
        value_block = block_rows[:, model_width:].reshape(step_rows, HEADS, HEAD_DIM)
        scores = (
            jnp.einsum("qhd,rhd->qhr", query_heads, key_block, preferred_element_type=jnp.float32)
            * score_scale
        )
        new_peak = jnp.maximum(peak_now, jnp.max(scores, axis=-1))
        rescale = jnp.exp(peak_now - new_peak)
        exponent = jnp.exp(scores - new_peak[..., None])
        denominator = denominator * rescale + jnp.sum(exponent, axis=-1)
        numerator = numerator * rescale[..., None] + jnp.einsum(
            "qhr,rhd->qhd",
            exponent.astype(jnp.bfloat16),
            value_block,
            preferred_element_type=jnp.float32,
        )
        return (new_peak, denominator, numerator)

    finished = lax.fori_loop(0, row_count // step_rows, one_block, starting)
    peak_final, denominator, numerator = finished
    attended = (
        (numerator / denominator[..., None]).astype(jnp.bfloat16).reshape(query_count, model_width)
    )
    return jnp.dot(attended, w_out, preferred_element_type=jnp.float32).astype(jnp.bfloat16)


def solution(mesh):
    return jax.shard_map(
        body,
        mesh=mesh,
        in_specs=(
            P(("region", "shard"), None, None),
            P(("region", "shard"), None),
            P(("region", "shard")),
            P(("region", "shard"), None),
            P(),
            P(),
            P(),
            P(),
            P(),
        ),
        out_specs=P(("region", "shard"), None),
        check_vma=False,
    )
```

profile of v0, /device:TPU:1, one launch (start us, length us, event | category | flops | bytes accessed | tf_op | source)
XLA Modules:
  0.0 421.8 jit_solution(3084942516669463617)
XLA Ops:
  6.5 0.8 fusion.38
  7.5 0.8 select_reduce_fusion
  8.4 0.7 fusion.42
  9.0 0.8 broadcast_in_dim.17
  9.8 10.0 %scatter_fusion = bf16[192,8,128]{2,1,0:T(8,128)(2,1)} fusion(bf16[192,8,128]{2,1,0:T(8,128)(2,1)} %broadcast_in_dim.17, s32[96]{0:T(128)S(1)} %fusion.42, bf16[96,8,128]{2,1,0:T(8,128)(2,1)} %param.11), kind=kCustom, calls=%fused_computation | custom fusion | bytes 590208 | tf_op jit(solution)/shard_map/scatter | solution.py:55
  19.8 12.9 %all-to-all-start = ((bf16[64,3,8,128]{3,2,1,0:T(8,128)(2,1)}), bf16[64,3,8,128]{3,2,1,0:T(8,128)(2,1)S(1)}, u32[]{:S(2)}, u32[]{:S(2)}) async-start(bf16[64,3,8,128]{3,2,1,0:T(8,128)(2,1)} %bitcast.7), calls=%async_computation | async-start | bytes 786432 | tf_op jit(solution)/shard_map/all_to_all | solution.py:61
  32.8 0.7 add_bitcast_fusion
  33.5 129.2 %all-gather = s32[64,96,2]{1,2,0:T(2,128)S(1)} all-gather(s32[1,96,2]{1,2,0:T(2,128)S(1)} %add_bitcast_fusion), channel_id=1, replica_groups=mesh['region'=8,'shard'=64] {'shard'}, dimensions={0}, use_global_device_ids=true | all-gather | bytes 49920 | tf_op jit(solution)/shard_map/all_gather | solution.py:31
  163.2 3.3 fusion.27
  166.8 0.8 fusion.34
  167.6 1.6 fusion.22
  170.9 124.8 %all-gather.1 = bf16[64,2,1536]{2,1,0:T(2,128)(2,1)S(1)} all-gather(bf16[1,2,1536]{2,1,0:T(2,128)(2,1)S(1)} %maximum_bitcast_fusion), channel_id=1, replica_groups=mesh['region'=8,'shard'=64] {'shard'}, dimensions={0}, use_global_device_ids=true | all-gather | bytes 399360 | tf_op jit(solution)/shard_map/all_gather | solution.py:82
  295.9 0.9 copy.46
  297.3 103.9 %all-gather.4.cloned.1.call-done = bf16[1024,1536]{0,1:T(8,128)(2,1)} async-done(((bf16[128,1536]{0,1:T(8,128)(2,1)}), bf16[1024,1536]{0,1:T(8,128)(2,1)}) %all-gather.4.cloned.1.call-update) | async-done | bytes 3145744 | tf_op jit(solution)/shard_map/all_gather | solution.py:83
  401.1 12.8 %while.18 = (s32[]{:T(128)}, f32[256,12]{0,1:T(8,128)S(1)}, f32[256,12]{0,1:T(8,128)S(1)}, f32[256,12,64]{0,2,1:T(8,128)S(1)}, bf16[1024,1536]{0,1:T(8,128)(2,1)...) while((s32[]{:T(128)}, f32[256,12]{0,1:T(8,128)S(1)}, ...), condition=%wide.region_11.12_spmd.clone, body=%wide.region_8.11_spmd.clone.sunk | while | flops 208223232 | bytes 13959363 | solution.py:108
  401.1 1.2 fusion.68
  403.6 0.8 fusion.71
  404.3 1.2 fusion.68
  406.7 0.8 fusion.71
  407.5 1.2 fusion.68
  409.9 0.8 fusion.71
  410.7 1.2 fusion.68
  413.1 0.8 fusion.71
  414.0 0.9 convolution_convert_fusion.1
  (59 shorter events, 7.9 us)
Async XLA Ops:
  6.5 163.6 %copy-start = (bf16[768,768]{1,0:T(8,128)(2,1)S(1)}, bf16[768,768]{1,0:T(8,128)(2,1)}, u32[]{:S(2)}) copy-start(bf16[768,768]{1,0:T(8,128)(2,1)} %param.17) | copy-start | bytes 3538948
  6.5 161.1 %copy-start.5 = (bf16[128,768]{1,0:T(8,128)(2,1)S(1)}, bf16[128,768]{1,0:T(8,128)(2,1)}, u32[]{:S(2)}) copy-start(bf16[128,768]{1,0:T(8,128)(2,1)} %param.15) | copy-start | bytes 589828
  19.8 147.8 %all-to-all-start = ((bf16[64,3,8,128]{3,2,1,0:T(8,128)(2,1)}), bf16[64,3,8,128]{3,2,1,0:T(8,128)(2,1)S(1)}, u32[]{:S(2)}, u32[]{:S(2)}) async-start(bf16[64,3,8,128]{3,2,1,0:T(8,128)(2,1)} %bitcast.7), calls=%async_computation | async-start | bytes 786432 | tf_op jit(solution)/shard_map/all_to_all | solution.py:61
  32.8 368.4 %all-gather.4.cloned.1.call-start = ((), (), s32[]{:S(2)}) async-start(), calls=%async_computation.1 | async-start | bytes 3538944 | tf_op jit(solution)/shard_map/all_gather | solution.py:83
  169.3 1.3 copy-start.4
  169.9 126.9 %copy-start.1 = (bf16[128,768]{1,0:T(8,128)(2,1)S(1)}, bf16[128,768]{1,0:T(8,128)(2,1)}, u32[]{:S(2)}) copy-start(bf16[128,768]{1,0:T(8,128)(2,1)} %param.18) | copy-start | bytes 589828
  170.0 126.9 %copy-start.3 = (bf16[256,128]{1,0:T(8,128)(2,1)S(1)}, bf16[256,128]{1,0:T(8,128)(2,1)}, u32[]{:S(2)}) copy-start(bf16[256,128]{1,0:T(8,128)(2,1)} %param.14) | copy-start | bytes 196612
  401.1 12.8 %copy-start.2 = (bf16[768,128]{1,0:T(8,128)(2,1)S(1)}, bf16[768,128]{1,0:T(8,128)(2,1)}, u32[]{:S(2)}) copy-start(bf16[768,128]{1,0:T(8,128)(2,1)} %param.19) | copy-start | bytes 589828
Sparse Core Ops, SparseCore 0:
  296.9 104.1 all-gather.3
where the time goes:
time: 423 us; the launch traced here: 422 us
  blocking collectives  254 us (60%)
  waiting for transfers between devices  104 us (25%)
  local copies, waits for them, and re-layouts  17.4 us (4%)
  between operations  13.6 us (3%)
  starting transfers between devices  13 us (3%)
  matrix products  10.4 us (2%)
  other arithmetic  9.21 us (2%)
    all_gather x1, blocking collectives, body(): lax.all_gather(jnp.stack([owner_shard, block_node], axis=1), 'shard', axi...  129 us
    all_gather x1, blocking collectives, body(): region_rows = lax.all_gather(anchor_rows, 'shard', axis=0, tiled=True)  125 us
    all_gather x1, waiting for transfers between devices, body(): key_values = lax.all_gather(region_rows, 'region', axis=0, tiled=True)  104 us
    all_to_all x1, starting transfers between devices, body(): lax.all_to_all(outgoing, 'shard', split_axis=0, concat_axis=0, tiled=True)  12.9 us
    scatter x1, local copies, waits for them, and re-layouts, body(): outgoing = jnp.zeros((shard_count * capacity, block_points, in_features),...  10 us
  transfers between devices with their start and end apart: 2, of which 1 were waited for; matrix products, arithmetic and copies ran while one was open for 1% of the time, Pallas kernels for 0%

commit v1 on v0

--- a/solution.py
+++ b/solution.py
@@ -28,8 +28,14 @@
     model_width = w_in.shape[1]
     capacity = max(2, 2 * block_count // shard_count)
     owner_shard = block_owner[:, 0]
-    routing = lax.all_gather(
-        jnp.stack([owner_shard, block_node], axis=1), "shard", axis=0, tiled=True
+    routing = jnp.concatenate(
+        lax.all_to_all(
+            jnp.stack([jnp.stack([owner_shard, block_node], axis=1)] * lax.axis_size("shard")),
+            "shard",
+            0,
+            0,
+        ),
+        axis=0,
     )
     routing = routing.reshape(shard_count, block_count, 2)
     every_owner = routing[:, :, 0]

time: 423 us -> 290 us (0.69)
  blocking collectives: 254 us -> 128 us
  waiting for transfers between devices: 104 us -> 86 us
  starting transfers between devices: 13 us -> 23.7 us
    all_gather x1 -> x0, blocking collectives: 129 us -> none  [body(): lax.all_gather(jnp.stack([owner_shard, block_node], axis=1), 'shard', axi...]
    all_gather x1, waiting for transfers between devices: 104 us -> 77.3 us  [body(): key_values = lax.all_gather(region_rows, 'region', axis=0, tiled=True)]
    all_to_all x0 -> x1, starting transfers between devices: none -> 12.9 us  [body(): lax.all_to_all(jnp.stack([jnp.stack([owner_shard, block_node], axis=1)] *...]
    all_to_all x1, waiting for transfers between devices: 0.01 us -> 8.69 us  [body(): lax.all_to_all(outgoing, 'shard', split_axis=0, concat_axis=0, tiled=True)]
  transfers between devices with their start and end apart: 2 -> 3, of which waited for: 1 -> 2; matrix products, arithmetic and copies ran while one was open for 1% -> 6% of each run, Pallas kernels for 0% -> 0%
where the time goes in v1:
time: 290 us; the launch traced here: 289 us
  blocking collectives  128 us (44%)
  waiting for transfers between devices  86 us (30%)
  starting transfers between devices  23.7 us (8%)
  local copies, waits for them, and re-layouts  18 us (6%)
  between operations  13.6 us (5%)
  matrix products  10.5 us (4%)
  other arithmetic  9.21 us (3%)
    all_gather x1, blocking collectives, body(): region_rows = lax.all_gather(anchor_rows, 'shard', axis=0, tiled=True)  128 us
    all_gather x1, waiting for transfers between devices, body(): key_values = lax.all_gather(region_rows, 'region', axis=0, tiled=True)  77.3 us
    all_to_all x1, starting transfers between devices, body(): lax.all_to_all(jnp.stack([jnp.stack([owner_shard, block_node], axis=1)] *...  12.9 us
    all_to_all x1, starting transfers between devices, body(): lax.all_to_all(outgoing, 'shard', split_axis=0, concat_axis=0, tiled=True)  10.8 us
    scatter x1, local copies, waits for them, and re-layouts, body(): outgoing = jnp.zeros((shard_count * capacity, block_points, in_features),...  10 us
    all_to_all x1, waiting for transfers between devices, body(): lax.all_to_all(outgoing, 'shard', split_axis=0, concat_axis=0, tiled=True)  8.69 us
  transfers between devices with their start and end apart: 3, of which 2 were waited for; matrix products, arithmetic and copies ran while one was open for 6% of the time, Pallas kernels for 0%

profile of v1, /device:TPU:1, one launch (start us, length us, event | category | flops | bytes accessed | tf_op | source)
XLA Modules:
  0.0 288.9 jit_solution(15293240421452261000)
XLA Ops:
  6.5 0.8 pad_add_fusion
  8.0 12.9 %all-to-all-start = ((s32[64,96,2]{1,2,0:T(2,128)}), s32[64,96,2]{1,2,0:T(2,128)S(1)}, u32[]{:S(2)}, u32[]{:S(2)}) async-start(s32[64,96,2]{1,2,0:T(2,128)} %stack.8), calls=%async_computation | async-start | bytes 131072 | tf_op jit(solution)/shard_map/all_to_all | solution.py:32
  20.9 0.7 fusion.38
  21.8 0.8 select_reduce_fusion
  23.3 0.8 broadcast_in_dim.17
  24.1 10.0 %scatter_fusion = bf16[192,8,128]{2,1,0:T(8,128)(2,1)} fusion(bf16[192,8,128]{2,1,0:T(8,128)(2,1)} %broadcast_in_dim.17, s32[96]{0:T(128)S(1)} %fusion.42, bf16[96,8,128]{2,1,0:T(8,128)(2,1)} %param.11), kind=kCustom, calls=%fused_computation | custom fusion | bytes 590208 | tf_op jit(solution)/shard_map/scatter | solution.py:61
  34.1 10.8 %all-to-all-start.1 = ((bf16[64,3,8,128]{3,2,1,0:T(8,128)(2,1)}), bf16[64,3,8,128]{3,2,1,0:T(8,128)(2,1)S(1)}, u32[]{:S(2)}, u32[]{:S(2)}) async-start(bf16[64,3,8,128]{3,2,1,0:T(8,128)(2,1)} %bitcast.6), calls=%async_computation.1 | async-start | bytes 786432 | tf_op jit(solution)/shard_map/all_to_all | solution.py:67
  45.4 3.3 %fusion.27 = s32[64,96]{0,1:T(8,128)S(1)} fusion(s32[64,96]{0,1:T(8,128)S(1)} %copy.42), kind=kOutput, calls=%fused_computation.33 | output fusion | flops 40101888 | bytes 49152 | tf_op jit(solution)/shard_map/jit(cumsum)/reduce_window_sum | solution.py:21
  49.0 0.8 fusion.34
  49.8 8.7 %all-to-all-done.1 = bf16[64,3,8,128]{3,2,1,0:T(8,128)(2,1)S(1)} async-done(((bf16[64,3,8,128]{3,2,1,0:T(8,128)(2,1)}), bf16[64,3,8,128]{3,2,1,0:T(8,128)(2,1)S(1)}, u32[]{:S(2)}, u32[]{:S(2)}) %all-to-all-start.1) | async-done | bytes 393248 | tf_op jit(solution)/shard_map/all_to_all | solution.py:67
  58.5 1.6 fusion.22
  61.8 127.5 %all-gather = bf16[64,2,1536]{2,1,0:T(2,128)(2,1)S(1)} all-gather(bf16[1,2,1536]{2,1,0:T(2,128)(2,1)S(1)} %maximum_bitcast_fusion), channel_id=1, replica_groups=mesh['region'=8,'shard'=64] {'shard'}, dimensions={0}, use_global_device_ids=true | all-gather | bytes 399360 | tf_op jit(solution)/shard_map/all_gather | solution.py:88
  189.5 0.9 copy.45
  190.9 77.3 %all-gather.3.cloned.1.call-done = bf16[1024,1536]{0,1:T(8,128)(2,1)} async-done(((bf16[128,1536]{0,1:T(8,128)(2,1)}), bf16[1024,1536]{0,1:T(8,128)(2,1)}) %all-gather.3.cloned.1.call-update) | async-done | bytes 3145744 | tf_op jit(solution)/shard_map/all_gather | solution.py:89
  268.2 12.8 %while.18 = (s32[]{:T(128)}, f32[256,12]{0,1:T(8,128)S(1)}, f32[256,12]{0,1:T(8,128)S(1)}, f32[256,12,64]{0,2,1:T(8,128)S(1)}, bf16[1024,1536]{0,1:T(8,128)(2,1)...) while((s32[]{:T(128)}, f32[256,12]{0,1:T(8,128)S(1)}, ...), condition=%wide.region_11.12_spmd.clone, body=%wide.region_8.11_spmd.clone.sunk | while | flops 208223232 | bytes 13959363 | solution.py:114
  268.2 1.2 fusion.68
  270.7 0.8 fusion.71
  271.5 1.2 fusion.68
  273.8 0.8 fusion.71
  274.6 1.2 fusion.68
  277.0 0.8 fusion.71
  277.8 1.2 fusion.68
  280.2 0.8 fusion.71
  281.1 0.9 convolution_convert_fusion.1
  (61 shorter events, 9.2 us)
Async XLA Ops:
  6.5 54.6 %copy-start = (bf16[768,768]{1,0:T(8,128)(2,1)S(1)}, bf16[768,768]{1,0:T(8,128)(2,1)}, u32[]{:S(2)}) copy-start(bf16[768,768]{1,0:T(8,128)(2,1)} %param.17) | copy-start | bytes 3538948
  6.5 52.0 %copy-start.5 = (bf16[128,768]{1,0:T(8,128)(2,1)S(1)}, bf16[128,768]{1,0:T(8,128)(2,1)}, u32[]{:S(2)}) copy-start(bf16[128,768]{1,0:T(8,128)(2,1)} %param.15) | copy-start | bytes 589828
  8.0 26.1 %all-to-all-start = ((s32[64,96,2]{1,2,0:T(2,128)}), s32[64,96,2]{1,2,0:T(2,128)S(1)}, u32[]{:S(2)}, u32[]{:S(2)}) async-start(s32[64,96,2]{1,2,0:T(2,128)} %stack.8), calls=%async_computation | async-start | bytes 131072 | tf_op jit(solution)/shard_map/all_to_all | solution.py:32
  34.1 24.4 %all-to-all-start.1 = ((bf16[64,3,8,128]{3,2,1,0:T(8,128)(2,1)}), bf16[64,3,8,128]{3,2,1,0:T(8,128)(2,1)S(1)}, u32[]{:S(2)}, u32[]{:S(2)}) async-start(bf16[64,3,8,128]{3,2,1,0:T(8,128)(2,1)} %bitcast.6), calls=%async_computation.1 | async-start | bytes 786432 | tf_op jit(solution)/shard_map/all_to_all | solution.py:67
  44.9 223.4 %all-gather.3.cloned.1.call-start = ((), (), s32[]{:S(2)}) async-start(), calls=%async_computation.2 | async-start | bytes 3538944 | tf_op jit(solution)/shard_map/all_gather | solution.py:89
  60.2 1.3 copy-start.4
  60.9 129.6 %copy-start.1 = (bf16[128,768]{1,0:T(8,128)(2,1)S(1)}, bf16[128,768]{1,0:T(8,128)(2,1)}, u32[]{:S(2)}) copy-start(bf16[128,768]{1,0:T(8,128)(2,1)} %param.18) | copy-start | bytes 589828
  60.9 129.6 %copy-start.3 = (bf16[256,128]{1,0:T(8,128)(2,1)S(1)}, bf16[256,128]{1,0:T(8,128)(2,1)}, u32[]{:S(2)}) copy-start(bf16[256,128]{1,0:T(8,128)(2,1)} %param.14) | copy-start | bytes 196612
  268.2 12.9 %copy-start.2 = (bf16[768,128]{1,0:T(8,128)(2,1)S(1)}, bf16[768,128]{1,0:T(8,128)(2,1)}, u32[]{:S(2)}) copy-start(bf16[768,128]{1,0:T(8,128)(2,1)} %param.19) | copy-start | bytes 589828
Sparse Core Ops, SparseCore 0:
  190.5 77.6 all-gather.2
